TPU v7x, 32 devices: a whole 2x2x4 slice. The times are simulated.
32 devices in a mesh: batch: 8 (over z, x), mp: 4 (over y, core).
Axes of the slice: x: 2, y: 2, z: 4, core: 2. Of those that a mesh axis runs over, the one named last changes fastest.
Arguments:
- tokens: bfloat16 [16, 2048, 768], P('batch', 'mp'), may hold values from -6 to 6
- cotangent: bfloat16 [16, 2048, 768], P('batch', 'mp'), may hold values from -6 to 6
- lengths: int32 [16], P('batch'), may hold values from 64 to 2048, as said below
- pre_attn_gain: bfloat16 [768], replicated, may hold values from 0.099609375 to 1.8984375
- pre_attn_bias: bfloat16 [768], replicated, may hold values from -3 to 3
- qkv_weight: bfloat16 [3, 768, 768], replicated, may hold values from -0.21875 to 0.21875
- conv_weight: bfloat16 [3, 3, 768], replicated, may hold values from -3 to 3
- out_weight: bfloat16 [768, 768], replicated, may hold values from -1.5 to 1.5
- pre_ffn_gain: bfloat16 [768], replicated, may hold values from 0.099609375 to 1.8984375
- pre_ffn_bias: bfloat16 [768], replicated, may hold values from -3 to 3
- up_weight: bfloat16 [768, 3072], replicated, may hold values from -0.21875 to 0.21875
- up_bias: bfloat16 [3072], replicated, may hold values from -3 to 3
- down_weight: bfloat16 [3072, 768], replicated, may hold values from -0.109375 to 0.109375
- down_bias: bfloat16 [768], replicated, may hold values from -3 to 3
Outputs:
- output: bfloat16 [16, 2048, 768], P('batch', 'mp')
- tokens_grad: bfloat16 [16, 2048, 768], P('batch', 'mp')
- pre_attn_gain_grad: float32 [768], P(('batch', 'mp'))
- pre_attn_bias_grad: float32 [768], P(('batch', 'mp'))
- qkv_weight_grad: float32 [3, 768, 768], P(None, 'batch', 'mp')
- conv_weight_grad: float32 [3, 3, 768], P(None, None, ('batch', 'mp'))
- out_weight_grad: float32 [768, 768], P(('batch', 'mp'))
- pre_ffn_gain_grad: float32 [768], P(('batch', 'mp'))
- pre_ffn_bias_grad: float32 [768], P(('batch', 'mp'))
- up_weight_grad: float32 [768, 3072], P(('batch', 'mp'))
- up_bias_grad: float32 [3072], P(('batch', 'mp'))
- down_weight_grad: float32 [3072, 768], P(('batch', 'mp'))
- down_bias_grad: float32 [768], P(('batch', 'mp'))
Inputs may be any that keep to these rules, and one draw needn't show every extreme that they name: `lengths`: real tokens of each sequence; positions at or past it are padding. Some sequence has 2048 in every draw.
All inputs are finite; a program needn't handle non-finite values.
Results may differ from a plain program's by a relative error of at most 0.014.
The roundings to bfloat16 on the way count: a program that leaves them out, or rounds other values in their place, can miss the bound.
Values may be sent and summed in bfloat16 or wider, within the bound.
No kernel may reach another device: no remote copies, remote signals or barrier semaphores. Data moves between devices by JAX's collectives and lax.ppermute only.
A program may use at most 320 MiB of HBM per device.

v0:
```python
import jax
import jax.numpy as jnp
from jax import lax
from jax.sharding import PartitionSpec as P

HEAD_DIM = 64
QBLOCK = 512
EPSILON = 1e-05
NEGATIVE = -1000000000.0


def norm_forward(values, norm_gain, offset):
    center = values - jnp.mean(values, axis=-1, keepdims=True)
    inv_std = lax.rsqrt(jnp.mean(center * center, axis=-1, keepdims=True) + EPSILON)
    scaled = center * inv_std
    return (scaled * norm_gain + offset, scaled, inv_std)


def norm_backward(grad_out, norm_gain, scaled, inv_std):
    weighted = grad_out * norm_gain
    return inv_std * (
        weighted
        - jnp.mean(weighted, axis=-1, keepdims=True)
        - scaled * jnp.mean(weighted * scaled, axis=-1, keepdims=True)
    )


def conv_forward(values, kernel):
    taps = kernel.shape[1]
    seq_len = values.shape[0]
    padded = jnp.pad(values, ((taps - 1, 0), (0, 0), (0, 0)))
    total_sum = jnp.zeros(values.shape, jnp.float32)
    for offset in range(taps):
        first = taps - 1 - offset
        total_sum = total_sum + kernel[:, offset, :] * padded[first : first + seq_len]
    return (total_sum, padded)


def conv_backward(grad_mixed, kernel, padded):
    taps = kernel.shape[1]
    seq_len = grad_mixed.shape[0]
    grad_padded = jnp.pad(grad_mixed, ((0, taps - 1), (0, 0), (0, 0)))
    grad_values = jnp.zeros(grad_mixed.shape, jnp.float32)
    kernel_grads = []
    for offset in range(taps):
        first = taps - 1 - offset
        grad_values = grad_values + kernel[:, offset, :] * grad_padded[offset : offset + seq_len]
        kernel_grads.append(jnp.sum(grad_mixed * padded[first : first + seq_len], axis=0))
    return (grad_values, jnp.stack(kernel_grads, axis=1))


def block_scores(block_q, key_heads, first, length, key_pos):
    scores = jnp.einsum(
        "qhd,khd->hqk", block_q, key_heads, preferred_element_type=jnp.float32
    ) * HEAD_DIM ** (-0.5)
    query_pos = first + jnp.arange(block_q.shape[0], dtype=jnp.int32)
    allowed = (key_pos[None, :] <= query_pos[:, None]) & (key_pos[None, :] < length)
    return jnp.where(allowed[None], scores, NEGATIVE)


def attend_forward(mixed_b, length):
    seq_len = mixed_b.shape[0]
    head_vals = mixed_b.reshape(seq_len, 3, -1, HEAD_DIM)
    queries = head_vals[:, 0]
    key_heads = head_vals[:, 1]
    values = head_vals[:, 2]
    key_pos = jnp.arange(seq_len, dtype=jnp.int32)
    out_parts = []
    log_totals = []
    for first in range(0, seq_len, QBLOCK):
        scores = block_scores(queries[first : first + QBLOCK], key_heads, first, length, key_pos)
        log_total = jax.nn.logsumexp(scores, axis=-1, keepdims=True)
        prob_block = jnp.exp(scores - log_total).astype(jnp.bfloat16)
        out_parts.append(
            jnp.einsum("hqk,khd->qhd", prob_block, values, preferred_element_type=jnp.float32)
        )
        log_totals.append(log_total)
    return (jnp.concatenate(out_parts, axis=0).reshape(seq_len, -1), log_totals)


def attend_backward(mixed_b, grad_heads, log_totals, length):
    seq_len = mixed_b.shape[0]
    head_vals = mixed_b.reshape(seq_len, 3, -1, HEAD_DIM)
    queries = head_vals[:, 0]
    key_heads = head_vals[:, 1]
    values = head_vals[:, 2]
    grad_out = grad_heads.reshape(seq_len, -1, HEAD_DIM)
    key_pos = jnp.arange(seq_len, dtype=jnp.int32)
    scale = HEAD_DIM ** (-0.5)
    query_parts = []
    grad_keys = jnp.zeros(key_heads.shape, jnp.float32)
    grad_values = jnp.zeros(values.shape, jnp.float32)
    for block_index, first in enumerate(range(0, seq_len, QBLOCK)):
        block_q = queries[first : first + QBLOCK]
        scores = block_scores(block_q, key_heads, first, length, key_pos)
        prob_block = jnp.exp(scores - log_totals[block_index])
        block_grad = grad_out[first : first + QBLOCK]
        grad_values = grad_values + jnp.einsum(
            "hqk,qhd->khd",
            prob_block.astype(jnp.bfloat16),
            block_grad,
            preferred_element_type=jnp.float32,
        )
        grad_probs = jnp.einsum(
            "qhd,khd->hqk", block_grad, values, preferred_element_type=jnp.float32
        )
        row_delta = jnp.sum(grad_probs * prob_block, axis=-1, keepdims=True)
        grad_scores = (prob_block * (grad_probs - row_delta)).astype(jnp.bfloat16)
        query_parts.append(
            jnp.einsum("hqk,khd->qhd", grad_scores, key_heads, preferred_element_type=jnp.float32)
            * scale
        )
        grad_keys = (
            grad_keys
            + jnp.einsum("hqk,qhd->khd", grad_scores, block_q, preferred_element_type=jnp.float32)
            * scale
        )
    grad_queries = jnp.concatenate(query_parts, axis=0)
    return jnp.stack([grad_queries, grad_keys, grad_values], axis=1).reshape(seq_len, 3, -1)


def on_device(
    tokens,
    cotangent,
    lengths,
    pre_attn_gain,
    pre_attn_bias,
    qkv_weight,
    conv_weight,
    out_weight,
    pre_ffn_gain,
    pre_ffn_bias,
    up_weight,
    up_bias,
    down_weight,
    down_bias,
):
    groups = lax.axis_size("mp")
    member = lax.axis_index("mp")
    batch_groups = lax.axis_size("batch")
    local_rows = tokens.shape[1]
    model_width = tokens.shape[2]
    head_cols = model_width // groups
    col_start = member * head_cols
    taps = conv_weight.shape[1]
    kernel_own = lax.dynamic_slice_in_dim(conv_weight, col_start, head_cols, 2).astype(jnp.float32)
    gain_attn = pre_attn_gain.astype(jnp.float32)
    bias_attn = pre_attn_bias.astype(jnp.float32)
    gain_ffn = pre_ffn_gain.astype(jnp.float32)
    bias_ffn = pre_ffn_bias.astype(jnp.float32)
    up_bias_f = up_bias.astype(jnp.float32)
    down_bias_f = down_bias.astype(jnp.float32)
    row_pos = member * local_rows + jnp.arange(local_rows, dtype=jnp.int32)
    qkv_grad_shape = (3, model_width, model_width)

    def one_batch(running, inputs):
        seq_rows, grad_rows, length = inputs
        rows_f = seq_rows.astype(jnp.float32)
        valid_rows = (row_pos < length)[:, None]
        normed, scaled_attn, inv_attn = norm_forward(rows_f, gain_attn, bias_attn)
        normed_b = normed.astype(jnp.bfloat16)
        local_proj = jnp.einsum(
            "td,cde->tce", normed_b, qkv_weight, preferred_element_type=jnp.float32
        ).astype(jnp.bfloat16)
        projected_b = lax.all_to_all(local_proj, "mp", split_axis=2, concat_axis=0, tiled=True)
        mixed_f, padded = conv_forward(projected_b.astype(jnp.float32), kernel_own)
        mixed_b = mixed_f.astype(jnp.bfloat16)
        heads_out, log_totals = attend_forward(mixed_b, length)
        heads_tok = lax.all_to_all(
            heads_out.astype(jnp.bfloat16), "mp", split_axis=0, concat_axis=1, tiled=True
        )
        attended = jnp.dot(heads_tok, out_weight, preferred_element_type=jnp.float32)
        residual = rows_f + attended
        normed_ffn, scaled_ffn, inv_ffn = norm_forward(residual, gain_ffn, bias_ffn)
        normed_ffn_b = normed_ffn.astype(jnp.bfloat16)
        hidden_pre = (
            jnp.dot(normed_ffn_b, up_weight, preferred_element_type=jnp.float32) + up_bias_f
        )
        relu_part = jnp.maximum(hidden_pre, 0.0)
        activated = jnp.square(relu_part).astype(jnp.bfloat16)
        ffn_out = jnp.dot(activated, down_weight, preferred_element_type=jnp.float32) + down_bias_f
        result = jnp.where(valid_rows, residual + ffn_out, 0.0).astype(jnp.bfloat16)
        grad_y = jnp.where(valid_rows, grad_rows.astype(jnp.float32), 0.0)
        grad_ffn = grad_y.astype(jnp.bfloat16)
        grad_down = jnp.einsum("tf,td->fd", activated, grad_ffn, preferred_element_type=jnp.float32)
        grad_down_bias = jnp.sum(grad_ffn.astype(jnp.float32), axis=0)
        grad_act = jnp.einsum(
            "td,fd->tf", grad_ffn, down_weight, preferred_element_type=jnp.float32
        )
        grad_pre = (2.0 * relu_part * grad_act).astype(jnp.bfloat16)
        grad_up = jnp.einsum(
            "td,tf->df", normed_ffn_b, grad_pre, preferred_element_type=jnp.float32
        )
        grad_up_bias = jnp.sum(grad_pre.astype(jnp.float32), axis=0)
        grad_normed_ffn = jnp.einsum(
            "tf,df->td", grad_pre, up_weight, preferred_element_type=jnp.float32
        )
        grad_gain_ffn = jnp.sum(grad_normed_ffn * scaled_ffn, axis=0)
        grad_bias_ffn = jnp.sum(grad_normed_ffn, axis=0)
        grad_residual = grad_y + norm_backward(grad_normed_ffn, gain_ffn, scaled_ffn, inv_ffn)
        grad_attended = grad_residual.astype(jnp.bfloat16)
        grad_out_w = jnp.einsum(
            "te,td->ed", heads_tok, grad_attended, preferred_element_type=jnp.float32
        )
        grad_heads_tok = jnp.einsum(
            "td,ed->te", grad_attended, out_weight, preferred_element_type=jnp.float32
        ).astype(jnp.bfloat16)
        grad_heads = lax.all_to_all(grad_heads_tok, "mp", split_axis=1, concat_axis=0, tiled=True)
        grad_mixed = attend_backward(mixed_b, grad_heads, log_totals, length)
        grad_proj, grad_conv = conv_backward(grad_mixed, kernel_own, padded)
        grad_proj_b = grad_proj.astype(jnp.bfloat16)
        grad_proj_tok = lax.all_to_all(grad_proj_b, "mp", split_axis=0, concat_axis=2, tiled=True)
        grad_qkv = jnp.einsum(
            "td,tce->cde", normed_b, grad_proj_tok, preferred_element_type=jnp.float32
        )
        grad_normed = jnp.einsum(
            "tce,cde->td", grad_proj_tok, qkv_weight, preferred_element_type=jnp.float32
        )
        grad_gain_attn = jnp.sum(grad_normed * scaled_attn, axis=0)
        grad_bias_attn = jnp.sum(grad_normed, axis=0)
        grad_tokens = grad_residual + norm_backward(grad_normed, gain_attn, scaled_attn, inv_attn)
        updates = (
            grad_gain_attn,
            grad_bias_attn,
            grad_qkv,
            grad_conv,
            grad_out_w,
            grad_gain_ffn,
            grad_bias_ffn,
            grad_up,
            grad_up_bias,
            grad_down,
            grad_down_bias,
        )
        running = jax.tree.map(jnp.add, running, updates)
        return (running, (result, grad_tokens.astype(jnp.bfloat16)))

    start_grads = (
        jnp.zeros((model_width,), jnp.float32),
        jnp.zeros((model_width,), jnp.float32),
        jnp.zeros(qkv_grad_shape, jnp.float32),
        jnp.zeros((3, taps, head_cols), jnp.float32),
        jnp.zeros(out_weight.shape, jnp.float32),
        jnp.zeros((model_width,), jnp.float32),
        jnp.zeros((model_width,), jnp.float32),
        jnp.zeros(up_weight.shape, jnp.float32),
        jnp.zeros(up_bias.shape, jnp.float32),
        jnp.zeros(down_weight.shape, jnp.float32),
        jnp.zeros((model_width,), jnp.float32),
    )
    running, outputs = lax.scan(one_batch, start_grads, (tokens, cotangent, lengths))
    conv_full = lax.dynamic_update_slice_in_dim(
        jnp.zeros((3, taps, model_width), jnp.float32), running[3], col_start, 2
    )
    rows_part = model_width // batch_groups
    qkv_flat = (
        running[2]
        .reshape(3, batch_groups, rows_part, groups, head_cols)
        .transpose(1, 3, 0, 2, 4)
        .reshape(batch_groups * groups * 3 * rows_part, head_cols)
    )
    summed = (
        lax.psum_scatter(running[0], ("batch", "mp"), scatter_dimension=0, tiled=True),
        lax.psum_scatter(running[1], ("batch", "mp"), scatter_dimension=0, tiled=True),
        lax.psum_scatter(qkv_flat, ("batch", "mp"), scatter_dimension=0, tiled=True),
        lax.psum_scatter(conv_full, ("batch", "mp"), scatter_dimension=2, tiled=True),
        lax.psum_scatter(running[4], ("batch", "mp"), scatter_dimension=0, tiled=True),
        lax.psum_scatter(running[5], ("batch", "mp"), scatter_dimension=0, tiled=True),
        lax.psum_scatter(running[6], ("batch", "mp"), scatter_dimension=0, tiled=True),
        lax.psum_scatter(running[7], ("batch", "mp"), scatter_dimension=0, tiled=True),
        lax.psum_scatter(running[8], ("batch", "mp"), scatter_dimension=0, tiled=True),
        lax.psum_scatter(running[9], ("batch", "mp"), scatter_dimension=0, tiled=True),
        lax.psum_scatter(running[10], ("batch", "mp"), scatter_dimension=0, tiled=True),
    )
    qkv_sum = summed[2].reshape(3, rows_part, head_cols)
    return (
        outputs[0],
        outputs[1],
        summed[0],
        summed[1],
        qkv_sum,
        summed[3],
        summed[4],
        summed[5],
        summed[6],
        summed[7],
        summed[8],
        summed[9],
        summed[10],
    )


def solution(mesh):
    in_specs = (
        P("batch", "mp", None),
        P("batch", "mp", None),
        P("batch"),
        P(),
        P(),
        P(),
        P(),
        P(),
        P(),
        P(),
        P(),
        P(),
        P(),
        P(),
    )
    out_specs = (
        P("batch", "mp", None),
        P("batch", "mp", None),
        P(("batch", "mp")),
        P(("batch", "mp")),
        P(None, "batch", "mp"),
        P(None, None, ("batch", "mp")),
        P(("batch", "mp"), None),
        P(("batch", "mp")),
        P(("batch", "mp")),
        P(("batch", "mp"), None),
        P(("batch", "mp")),
        P(("batch", "mp"), None),
        P(("batch", "mp")),
    )
    return jax.shard_map(
        on_device, mesh=mesh, in_specs=in_specs, out_specs=out_specs, check_vma=False
    )
```

profile of v0, /device:TPU:0, one launch (start us, length us, event | category | flops | bytes accessed | tf_op | source)
XLA Modules:
  0.0 1405.1 jit_solution(3746548389037983586)
XLA Ops:
  13.4 859.4 %while.37 = (s32[]{:T(128)}, f32[768]{0:T(1024)}, f32[768]{0:T(1024)}, f32[3,768,768]{1,2,0:T(8,128)}, f32[3,3,192]{2,1,0:T(4,128)}, /*index=5*/f32[768,768]{1,0...) while((s32[]{:T(128)}, f32[768]{0:T(1024)}, ...), condition=%wide.region_30.31_spmd.clone, body=%wide.region_0.30_spmd.clone.sunk | while | flops 31852625920 | bytes 1296953600 | solution.py:251
  37.0 30.4 %all-to-all-done = bf16[512,3,768]{0,1,2:T(4,128)(2,1)} async-done(((bf16[512,3,768]{0,1,2:T(4,128)(2,1)}), bf16[512,3,768]{0,1,2:T(4,128)(2,1)}, u32[]{:S(2)}, u32[]{:S(2)}) %all-to-all-start) | async-done | bytes 2359328 | tf_op jit(solution)/shard_map/while/body/eval_jaxpr/all_to_all | solution.py:165
  161.4 10.9 all-to-all-done.1
  227.4 11.6 multiply_reduce_fusion.19
  287.0 10.3 multiply_reduce_fusion.22
  305.7 9.8 multiply_convert_fusion.19
  318.3 9.9 multiply_convert_fusion.18
  370.1 9.5 select_add_fusion.22
  392.6 25.7 %all-to-all-done.3 = bf16[2048,3,192]{2,1,0:T(4,128)(2,1)} async-done(((bf16[2048,3,192]{2,1,0:T(4,128)(2,1)}), bf16[2048,3,192]{2,1,0:T(4,128)(2,1)}, u32[]{:S(2)}, u32[]{:S(2)}) %all-to-all-start.3) | async-done | bytes 2359328 | tf_op jit(solution)/shard_map/while/body/eval_jaxpr/all_to_all | solution.py:212
  463.4 29.8 %all-to-all-done = bf16[512,3,768]{0,1,2:T(4,128)(2,1)} async-done(((bf16[512,3,768]{0,1,2:T(4,128)(2,1)}), bf16[512,3,768]{0,1,2:T(4,128)(2,1)}, u32[]{:S(2)}, u32[]{:S(2)}) %all-to-all-start) | async-done | bytes 2359328 | tf_op jit(solution)/shard_map/while/body/eval_jaxpr/all_to_all | solution.py:165
  587.2 10.9 all-to-all-done.1
  657.4 11.6 multiply_reduce_fusion.19
  716.9 10.3 multiply_reduce_fusion.22
  735.7 9.8 multiply_convert_fusion.19
  748.3 9.9 multiply_convert_fusion.18
  800.1 12.3 select_add_fusion.22
  825.3 22.9 %all-to-all-done.3 = bf16[2048,3,192]{2,1,0:T(4,128)(2,1)} async-done(((bf16[2048,3,192]{2,1,0:T(4,128)(2,1)}), bf16[2048,3,192]{2,1,0:T(4,128)(2,1)}, u32[]{:S(2)}, u32[]{:S(2)}) %all-to-all-start.3) | async-done | bytes 2359328 | tf_op jit(solution)/shard_map/while/body/eval_jaxpr/all_to_all | solution.py:212
  872.9 10.4 reshape.455
  883.3 10.2 copy.74
  895.2 41.7 %all-reduce.9 = (f32[768]{0:T(1024)S(1)}, f32[768]{0:T(1024)S(1)}, f32[3,3,768]{2,1,0:T(4,128)S(1)}, f32[768]{0:T(1024)S(1)}, f32[768]{0:T(1024)S(1)}, /*index=5*/f32[3072]{0:T(1024)S(1)}, f32[768]{0:T(1024)S(1)}) all-reduce(f32[768]{0:T(1024)S(1)} %copy-done.70, ...), channel_id=2, replica_groups=mesh['batch'=8,'mp'=4] {'batch','mp'}, use_global_device_ids=true, to_apply=%region_31.32.clone | all-reduce | flops 13824 | bytes 110592
  941.1 32.0 %reduce-scatter.8.cloned.1.call-done = f32[24,768]{1,0:T(8,128)} async-done(((f32[768,768]{1,0:T(8,128)}), f32[24,768]{1,0:T(8,128)}) %reduce-scatter.8.cloned.1.call-update) | async-done | bytes 73744 | tf_op jit(solution)/shard_map/reduce_scatter | solution.py:267
  973.1 142.0 %reduce-scatter.6.cloned.1.call-done = f32[288,192]{1,0:T(8,128)} async-done(((f32[9216,192]{1,0:T(8,128)}), f32[288,192]{1,0:T(8,128)}) %reduce-scatter.6.cloned.1.call-update) | async-done | bytes 221200 | tf_op jit(solution)/shard_map/reduce_scatter | solution.py:265
  1115.1 141.1 %reduce-scatter.10.cloned.1.call-done = f32[24,3072]{1,0:T(8,128)} async-done(((f32[768,3072]{1,0:T(8,128)}), f32[24,3072]{1,0:T(8,128)}) %reduce-scatter.10.cloned.1.call-update) | async-done | bytes 294928 | tf_op jit(solution)/shard_map/reduce_scatter | solution.py:270
  1256.3 142.0 %reduce-scatter.12.cloned.1.call-done = f32[96,768]{1,0:T(8,128)} async-done(((f32[3072,768]{1,0:T(8,128)}), f32[96,768]{1,0:T(8,128)}) %reduce-scatter.12.cloned.1.call-update) | async-done | bytes 294928 | tf_op jit(solution)/shard_map/reduce_scatter | solution.py:272
  (620 shorter events, 628.9 us)
Async XLA Ops:
  7.2 965.9 %reduce-scatter.8.cloned.1.call-start = ((), (), s32[]{:S(2)}) async-start(), calls=%async_computation.9 | async-start | bytes 2433024 | tf_op jit(solution)/shard_map/reduce_scatter | solution.py:267
  13.4 188.4 %copy-start.72 = (f32[768]{0:T(1024)}, f32[768]{0:T(1024)S(1)}, u32[]{:S(2)}) copy-start(f32[768]{0:T(1024)S(1)} %get-tuple-element.969) | copy-start | bytes 9220 | tf_op jit(solution)/shard_map/while
  13.4 196.3 %copy-start.37 = (f32[768]{0:T(1024)}, f32[768]{0:T(1024)S(1)}, u32[]{:S(2)}) copy-start(f32[768]{0:T(1024)S(1)} %get-tuple-element.964) | copy-start | bytes 9220 | tf_op jit(solution)/shard_map/while
  13.4 196.3 %copy-start.39 = (f32[768]{0:T(1024)}, f32[768]{0:T(1024)S(1)}, u32[]{:S(2)}) copy-start(f32[768]{0:T(1024)S(1)} %get-tuple-element.965) | copy-start | bytes 9220 | tf_op jit(solution)/shard_map/while
  24.9 42.4 %all-to-all-start = ((bf16[512,3,768]{0,1,2:T(4,128)(2,1)}), bf16[512,3,768]{0,1,2:T(4,128)(2,1)}, u32[]{:S(2)}, u32[]{:S(2)}) async-start(bf16[512,3,768]{0,1,2:T(4,128)(2,1)} %copy.93), calls=%async_computation | async-start | bytes 6291456 | tf_op jit(solution)/shard_map/while/body/eval_jaxpr/all_to_all | solution.py:165
  37.0 73.1 %copy-start.6 = (pred[512,2048]{1,0:T(8,128)(4,1)}, pred[512,2048]{1,0:T(8,128)(4,1)S(1)}, u32[]{:S(2)}) copy-start(pred[512,2048]{1,0:T(8,128)(4,1)S(1)} %get-tuple-element.837) | copy-start | bytes 3145732 | tf_op jit(solution)/shard_map/while
  37.0 92.6 %copy-start.9 = (pred[512,2048]{1,0:T(8,128)(4,1)}, pred[512,2048]{1,0:T(8,128)(4,1)S(1)}, u32[]{:S(2)}) copy-start(pred[512,2048]{1,0:T(8,128)(4,1)S(1)} %get-tuple-element.834) | copy-start | bytes 3145732 | tf_op jit(solution)/shard_map/while
  37.0 111.7 %copy-start.10 = (pred[512,2048]{1,0:T(8,128)(4,1)}, pred[512,2048]{1,0:T(8,128)(4,1)S(1)}, u32[]{:S(2)}) copy-start(pred[512,2048]{1,0:T(8,128)(4,1)S(1)} %get-tuple-element.831) | copy-start | bytes 3145732 | tf_op jit(solution)/shard_map/while
  156.8 15.5 %all-to-all-start.1 = ((bf16[4,512,192]{1,2,0:T(8,128)(2,1)}), bf16[4,512,192]{1,2,0:T(8,128)(2,1)S(1)}, u32[]{:S(2)}, u32[]{:S(2)}) async-start(bf16[4,512,192]{1,2,0:T(8,128)(2,1)} %copy.96), calls=%async_computation.1 | async-start | bytes 1572864 | tf_op jit(solution)/shard_map/while/body/eval_jaxpr/all_to_all | solution.py:169
  197.4 20.2 %all-to-all-start.2 = ((bf16[512,4,192]{0,2,1:T(8,128)(2,1)}), bf16[512,4,192]{0,2,1:T(8,128)(2,1)}, u32[]{:S(2)}, u32[]{:S(2)}) async-start(bf16[512,4,192]{0,2,1:T(8,128)(2,1)} %bitcast.484), calls=%async_computation.2 | async-start | bytes 1572864 | tf_op jit(solution)/shard_map/while/body/eval_jaxpr/all_to_all | solution.py:208
  364.8 53.4 %all-to-all-start.3 = ((bf16[2048,3,192]{2,1,0:T(4,128)(2,1)}), bf16[2048,3,192]{2,1,0:T(4,128)(2,1)}, u32[]{:S(2)}, u32[]{:S(2)}) async-start(bf16[2048,3,192]{2,1,0:T(4,128)(2,1)} %copy.98), calls=%async_computation.3 | async-start | bytes 8388608 | tf_op jit(solution)/shard_map/while/body/eval_jaxpr/all_to_all | solution.py:212
  439.8 187.8 %copy-start.72 = (f32[768]{0:T(1024)}, f32[768]{0:T(1024)S(1)}, u32[]{:S(2)}) copy-start(f32[768]{0:T(1024)S(1)} %get-tuple-element.969) | copy-start | bytes 9220 | tf_op jit(solution)/shard_map/while
  439.8 195.7 %copy-start.37 = (f32[768]{0:T(1024)}, f32[768]{0:T(1024)S(1)}, u32[]{:S(2)}) copy-start(f32[768]{0:T(1024)S(1)} %get-tuple-element.964) | copy-start | bytes 9220 | tf_op jit(solution)/shard_map/while
  439.8 195.7 %copy-start.39 = (f32[768]{0:T(1024)}, f32[768]{0:T(1024)S(1)}, u32[]{:S(2)}) copy-start(f32[768]{0:T(1024)S(1)} %get-tuple-element.965) | copy-start | bytes 9220 | tf_op jit(solution)/shard_map/while
  451.4 41.8 %all-to-all-start = ((bf16[512,3,768]{0,1,2:T(4,128)(2,1)}), bf16[512,3,768]{0,1,2:T(4,128)(2,1)}, u32[]{:S(2)}, u32[]{:S(2)}) async-start(bf16[512,3,768]{0,1,2:T(4,128)(2,1)} %copy.93), calls=%async_computation | async-start | bytes 6291456 | tf_op jit(solution)/shard_map/while/body/eval_jaxpr/all_to_all | solution.py:165
  463.4 91.9 %copy-start.9 = (pred[512,2048]{1,0:T(8,128)(4,1)}, pred[512,2048]{1,0:T(8,128)(4,1)S(1)}, u32[]{:S(2)}) copy-start(pred[512,2048]{1,0:T(8,128)(4,1)S(1)} %get-tuple-element.834) | copy-start | bytes 3145732 | tf_op jit(solution)/shard_map/while
  463.4 111.1 %copy-start.10 = (pred[512,2048]{1,0:T(8,128)(4,1)}, pred[512,2048]{1,0:T(8,128)(4,1)S(1)}, u32[]{:S(2)}) copy-start(pred[512,2048]{1,0:T(8,128)(4,1)S(1)} %get-tuple-element.831) | copy-start | bytes 3145732 | tf_op jit(solution)/shard_map/while
  582.7 15.5 %all-to-all-start.1 = ((bf16[4,512,192]{1,2,0:T(8,128)(2,1)}), bf16[4,512,192]{1,2,0:T(8,128)(2,1)S(1)}, u32[]{:S(2)}, u32[]{:S(2)}) async-start(bf16[4,512,192]{1,2,0:T(8,128)(2,1)} %copy.96), calls=%async_computation.1 | async-start | bytes 1572864 | tf_op jit(solution)/shard_map/while/body/eval_jaxpr/all_to_all | solution.py:169
  623.3 24.3 %all-to-all-start.2 = ((bf16[512,4,192]{0,2,1:T(8,128)(2,1)}), bf16[512,4,192]{0,2,1:T(8,128)(2,1)}, u32[]{:S(2)}, u32[]{:S(2)}) async-start(bf16[512,4,192]{0,2,1:T(8,128)(2,1)} %bitcast.484), calls=%async_computation.2 | async-start | bytes 1572864 | tf_op jit(solution)/shard_map/while/body/eval_jaxpr/all_to_all | solution.py:208
  794.8 53.4 %all-to-all-start.3 = ((bf16[2048,3,192]{2,1,0:T(4,128)(2,1)}), bf16[2048,3,192]{2,1,0:T(4,128)(2,1)}, u32[]{:S(2)}, u32[]{:S(2)}) async-start(bf16[2048,3,192]{2,1,0:T(4,128)(2,1)} %copy.98), calls=%async_computation.3 | async-start | bytes 8388608 | tf_op jit(solution)/shard_map/while/body/eval_jaxpr/all_to_all | solution.py:212
  872.8 242.3 %reduce-scatter.6.cloned.1.call-start = ((), (), s32[]{:S(2)}) async-start(), calls=%async_computation.8 | async-start | bytes 9732096 | tf_op jit(solution)/shard_map/reduce_scatter | solution.py:265
  893.5 362.8 %reduce-scatter.10.cloned.1.call-start = ((), (), s32[]{:S(2)}) async-start(), calls=%async_computation.10 | async-start | bytes 9732096 | tf_op jit(solution)/shard_map/reduce_scatter | solution.py:270
  894.2 504.0 %reduce-scatter.12.cloned.1.call-start = ((), (), s32[]{:S(2)}) async-start(), calls=%async_computation.11 | async-start | bytes 9732096 | tf_op jit(solution)/shard_map/reduce_scatter | solution.py:272
  894.3 504.0 %copy-start.1 = (bf16[3,3,768]{2,1,0:T(4,128)(2,1)S(1)}, bf16[3,3,768]{2,1,0:T(4,128)(2,1)}, u32[]{:S(2)}) copy-start(bf16[3,3,768]{2,1,0:T(4,128)(2,1)} %param.22) | copy-start | bytes 41476
  (170 other events, 1678.6 us)
Sparse Core Ops, SparseCore 0:
  872.9 100.1 reduce-scatter.7
  980.6 134.4 reduce-scatter.5
  1121.6 134.6 reduce-scatter.9
  1263.6 134.5 reduce-scatter.11
where the time goes:
time: 1410 us
  waiting for transfers between devices  589 us (42%)
  matrix products  409 us (29%)
  other arithmetic  180 us (13%)
  local copies, waits for them, and re-layouts  127 us (9%)
  blocking collectives  41.7 us (3%)
  starting transfers between devices  36.8 us (3%)
  between operations  14.4 us (1%)
    reduce_scatter x1, waiting for transfers between devices, on_device(): lax.psum_scatter(qkv_flat, ('batch', 'mp'), scatter_dimension=0, tiled=True)  142 us
    reduce_scatter x1, waiting for transfers between devices, on_device(): lax.psum_scatter(running[9], ('batch', 'mp'), scatter_dimension=0, tiled=...  142 us
    reduce_scatter x1, waiting for transfers between devices, on_device(): lax.psum_scatter(running[7], ('batch', 'mp'), scatter_dimension=0, tiled=...  141 us
    dot_general x8, matrix products, attend_backward(): jnp.einsum('qhd,khd->hqk', block_grad, values, preferred_element_type=jnp...  80.2 us
    convert_element_type x8, other arithmetic, attend_backward(): grad_scores = (prob_block * (grad_probs - row_delta)).astype(jnp.bfloat16)  71.2 us
    all_to_all x2, waiting for transfers between devices, one_batch(): lax.all_to_all(local_proj, 'mp', split_axis=2, concat_axis=0, tiled=True)  60.2 us
    dot_general x8, matrix products, attend_backward(): jnp.einsum('hqk,qhd->khd', prob_block.astype(jnp.bfloat16), block_grad, p...  59.4 us
    reduce_sum x8, other arithmetic, attend_forward(): log_total = jax.nn.logsumexp(scores, axis=-1, keepdims=True)  54.1 us
  transfers between devices with their start and end apart: 12, of which 10 were waited for; matrix products, arithmetic and copies ran while one was open for 9% of the time, Pallas kernels for 0%

commit v1 on v0

--- a/solution.py
+++ b/solution.py
@@ -209,7 +209,12 @@
         grad_mixed = attend_backward(mixed_b, grad_heads, log_totals, length)
         grad_proj, grad_conv = conv_backward(grad_mixed, kernel_own, padded)
         grad_proj_b = grad_proj.astype(jnp.bfloat16)
-        grad_proj_tok = lax.all_to_all(grad_proj_b, "mp", split_axis=0, concat_axis=2, tiled=True)
+        grad_proj_tok = jnp.concatenate(
+            lax.all_to_all(
+                jnp.stack(jnp.split(grad_proj_b, lax.axis_size("mp"), axis=0)), "mp", 0, 0
+            ),
+            axis=2,
+        )
         grad_qkv = jnp.einsum(
             "td,tce->cde", normed_b, grad_proj_tok, preferred_element_type=jnp.float32
         )

time: 1410 us -> 1340 us (0.950)
  waiting for transfers between devices: 589 us -> 550 us
  local copies, waits for them, and re-layouts: 127 us -> 100 us
    all_to_all x2, waiting for transfers between devices: 48.6 us -> 8.67 us  [one_batch(): lax.all_to_all(jnp.stack(jnp.split(grad_proj_b, lax.axis_size('mp'), axis...]
    all_to_all x2 -> x0, local copies, waits for them, and re-layouts: 14.7 us -> none  [one_batch(): lax.all_to_all(grad_proj_b, 'mp', split_axis=0, concat_axis=2, tiled=True)]
where the time goes in v1:
time: 1340 us
  waiting for transfers between devices  550 us (41%)
  matrix products  411 us (31%)
  other arithmetic  178 us (13%)
  local copies, waits for them, and re-layouts  100 us (7%)
  blocking collectives  41.7 us (3%)
  starting transfers between devices  35.8 us (3%)
  between operations  14.4 us (1%)
    reduce_scatter x1, waiting for transfers between devices, on_device(): lax.psum_scatter(qkv_flat, ('batch', 'mp'), scatter_dimension=0, tiled=True)  142 us
    reduce_scatter x1, waiting for transfers between devices, on_device(): lax.psum_scatter(running[9], ('batch', 'mp'), scatter_dimension=0, tiled=...  142 us
    reduce_scatter x1, waiting for transfers between devices, on_device(): lax.psum_scatter(running[7], ('batch', 'mp'), scatter_dimension=0, tiled=...  141 us
    dot_general x8, matrix products, attend_backward(): jnp.einsum('qhd,khd->hqk', block_grad, values, preferred_element_type=jnp...  80.2 us
    convert_element_type x8, other arithmetic, attend_backward(): grad_scores = (prob_block * (grad_probs - row_delta)).astype(jnp.bfloat16)  71.2 us
    all_to_all x2, waiting for transfers between devices, one_batch(): lax.all_to_all(local_proj, 'mp', split_axis=2, concat_axis=0, tiled=True)  61.6 us
    dot_general x8, matrix products, attend_backward(): jnp.einsum('hqk,qhd->khd', prob_block.astype(jnp.bfloat16), block_grad, p...  59.4 us
    reduce_sum x8, other arithmetic, attend_forward(): log_total = jax.nn.logsumexp(scores, axis=-1, keepdims=True)  54.1 us
  transfers between devices with their start and end apart: 12, of which 10 were waited for; matrix products, arithmetic and copies ran while one was open for 9% of the time, Pallas kernels for 0%

profile of v1, /device:TPU:0, one launch (start us, length us, event | category | flops | bytes accessed | tf_op | source)
XLA Modules:
  0.0 1338.9 jit_solution(11107977282937041646)
XLA Ops:
  11.6 794.9 %while.37 = (s32[]{:T(128)}, f32[768]{0:T(1024)}, f32[768]{0:T(1024)}, f32[3,768,768]{1,2,0:T(8,128)}, f32[3,3,192]{2,1,0:T(4,128)}, /*index=5*/f32[768,768]{1,0...) while((s32[]{:T(128)}, f32[768]{0:T(1024)}, ...), condition=%wide.region_30.31_spmd.clone, body=%wide.region_0.30_spmd.clone.sunk | while | flops 31856164864 | bytes 1239124352 | solution.py:256
  34.5 31.1 %all-to-all-done = bf16[512,3,768]{0,1,2:T(4,128)(2,1)} async-done(((bf16[512,3,768]{0,1,2:T(4,128)(2,1)}), bf16[512,3,768]{0,1,2:T(4,128)(2,1)}, u32[]{:S(2)}, u32[]{:S(2)}) %all-to-all-start) | async-done | bytes 2359328 | tf_op jit(solution)/shard_map/while/body/eval_jaxpr/all_to_all | solution.py:165
  159.1 10.9 all-to-all-done.1
  225.1 11.6 multiply_reduce_fusion.19
  268.8 9.3 multiply_reduce_fusion.21
  284.7 10.3 multiply_reduce_fusion.22
  303.4 9.8 multiply_convert_fusion.19
  316.0 9.9 multiply_convert_fusion.18
  361.2 9.5 select_add_fusion.22
  427.6 30.5 %all-to-all-done = bf16[512,3,768]{0,1,2:T(4,128)(2,1)} async-done(((bf16[512,3,768]{0,1,2:T(4,128)(2,1)}), bf16[512,3,768]{0,1,2:T(4,128)(2,1)}, u32[]{:S(2)}, u32[]{:S(2)}) %all-to-all-start) | async-done | bytes 2359328 | tf_op jit(solution)/shard_map/while/body/eval_jaxpr/all_to_all | solution.py:165
  551.5 10.9 all-to-all-done.1
  621.7 11.6 multiply_reduce_fusion.19
  665.3 9.3 multiply_reduce_fusion.21
  681.2 10.3 multiply_reduce_fusion.22
  700.0 9.8 multiply_convert_fusion.19
  712.6 9.9 multiply_convert_fusion.18
  757.8 12.3 select_add_fusion.22
  806.6 10.4 reshape.467
  817.0 10.1 copy.60
  828.9 41.7 %all-reduce.9 = (f32[768]{0:T(1024)S(1)}, f32[768]{0:T(1024)S(1)}, f32[3,3,768]{2,1,0:T(4,128)S(1)}, f32[768]{0:T(1024)S(1)}, f32[768]{0:T(1024)S(1)}, /*index=5*/f32[3072]{0:T(1024)S(1)}, f32[768]{0:T(1024)S(1)}) all-reduce(f32[768]{0:T(1024)S(1)} %copy-done.74, ...), channel_id=2, replica_groups=mesh['batch'=8,'mp'=4] {'batch','mp'}, use_global_device_ids=true, to_apply=%region_31.32.clone | all-reduce | flops 13824 | bytes 110592
  874.8 32.0 %reduce-scatter.8.cloned.1.call-done = f32[24,768]{1,0:T(8,128)} async-done(((f32[768,768]{1,0:T(8,128)}), f32[24,768]{1,0:T(8,128)}) %reduce-scatter.8.cloned.1.call-update) | async-done | bytes 73744 | tf_op jit(solution)/shard_map/reduce_scatter | solution.py:272
  906.8 142.2 %reduce-scatter.6.cloned.1.call-done = f32[288,192]{1,0:T(8,128)} async-done(((f32[9216,192]{1,0:T(8,128)}), f32[288,192]{1,0:T(8,128)}) %reduce-scatter.6.cloned.1.call-update) | async-done | bytes 221200 | tf_op jit(solution)/shard_map/reduce_scatter | solution.py:270
  1049.0 141.1 %reduce-scatter.10.cloned.1.call-done = f32[24,3072]{1,0:T(8,128)} async-done(((f32[768,3072]{1,0:T(8,128)}), f32[24,3072]{1,0:T(8,128)}) %reduce-scatter.10.cloned.1.call-update) | async-done | bytes 294928 | tf_op jit(solution)/shard_map/reduce_scatter | solution.py:275
  1190.1 141.9 %reduce-scatter.12.cloned.1.call-done = f32[96,768]{1,0:T(8,128)} async-done(((f32[3072,768]{1,0:T(8,128)}), f32[96,768]{1,0:T(8,128)}) %reduce-scatter.12.cloned.1.call-update) | async-done | bytes 294928 | tf_op jit(solution)/shard_map/reduce_scatter | solution.py:277
  (628 shorter events, 591.1 us)
Async XLA Ops:
  7.2 899.6 %reduce-scatter.8.cloned.1.call-start = ((), (), s32[]{:S(2)}) async-start(), calls=%async_computation.9 | async-start | bytes 2433024 | tf_op jit(solution)/shard_map/reduce_scatter | solution.py:272
  11.6 187.9 %copy-start.76 = (f32[768]{0:T(1024)}, f32[768]{0:T(1024)S(1)}, u32[]{:S(2)}) copy-start(f32[768]{0:T(1024)S(1)} %get-tuple-element.981) | copy-start | bytes 9220 | tf_op jit(solution)/shard_map/while
  11.6 195.8 %copy-start.35 = (f32[768]{0:T(1024)}, f32[768]{0:T(1024)S(1)}, u32[]{:S(2)}) copy-start(f32[768]{0:T(1024)S(1)} %get-tuple-element.976) | copy-start | bytes 9220 | tf_op jit(solution)/shard_map/while
  11.6 195.7 %copy-start.37 = (f32[768]{0:T(1024)}, f32[768]{0:T(1024)S(1)}, u32[]{:S(2)}) copy-start(f32[768]{0:T(1024)S(1)} %get-tuple-element.977) | copy-start | bytes 9220 | tf_op jit(solution)/shard_map/while
  23.2 42.4 %all-to-all-start = ((bf16[512,3,768]{0,1,2:T(4,128)(2,1)}), bf16[512,3,768]{0,1,2:T(4,128)(2,1)}, u32[]{:S(2)}, u32[]{:S(2)}) async-start(bf16[512,3,768]{0,1,2:T(4,128)(2,1)} %copy.76), calls=%async_computation | async-start | bytes 6291456 | tf_op jit(solution)/shard_map/while/body/eval_jaxpr/all_to_all | solution.py:165
  34.5 73.4 %copy-start.6 = (pred[512,2048]{1,0:T(8,128)(4,1)}, pred[512,2048]{1,0:T(8,128)(4,1)S(1)}, u32[]{:S(2)}) copy-start(pred[512,2048]{1,0:T(8,128)(4,1)S(1)} %get-tuple-element.845) | copy-start | bytes 3145732 | tf_op jit(solution)/shard_map/while
  34.5 92.7 %copy-start.9 = (pred[512,2048]{1,0:T(8,128)(4,1)}, pred[512,2048]{1,0:T(8,128)(4,1)S(1)}, u32[]{:S(2)}) copy-start(pred[512,2048]{1,0:T(8,128)(4,1)S(1)} %get-tuple-element.842) | copy-start | bytes 3145732 | tf_op jit(solution)/shard_map/while
  34.5 111.8 %copy-start.10 = (pred[512,2048]{1,0:T(8,128)(4,1)}, pred[512,2048]{1,0:T(8,128)(4,1)S(1)}, u32[]{:S(2)}) copy-start(pred[512,2048]{1,0:T(8,128)(4,1)S(1)} %get-tuple-element.839) | copy-start | bytes 3145732 | tf_op jit(solution)/shard_map/while
  154.5 15.5 %all-to-all-start.1 = ((bf16[4,512,192]{1,2,0:T(8,128)(2,1)}), bf16[4,512,192]{1,2,0:T(8,128)(2,1)S(1)}, u32[]{:S(2)}, u32[]{:S(2)}) async-start(bf16[4,512,192]{1,2,0:T(8,128)(2,1)} %copy.79), calls=%async_computation.1 | async-start | bytes 1572864 | tf_op jit(solution)/shard_map/while/body/eval_jaxpr/all_to_all | solution.py:169
  195.1 20.2 %all-to-all-start.2 = ((bf16[512,4,192]{0,2,1:T(8,128)(2,1)}), bf16[512,4,192]{0,2,1:T(8,128)(2,1)}, u32[]{:S(2)}, u32[]{:S(2)}) async-start(bf16[512,4,192]{0,2,1:T(8,128)(2,1)} %bitcast.489), calls=%async_computation.2 | async-start | bytes 1572864 | tf_op jit(solution)/shard_map/while/body/eval_jaxpr/all_to_all | solution.py:208
  356.4 33.3 %all-to-all-start.3 = ((bf16[4,512,3,192]{1,3,2,0:T(8,128)(2,1)}), bf16[4,512,3,192]{1,3,2,0:T(8,128)(2,1)}, u32[]{:S(2)}, u32[]{:S(2)}) async-start(bf16[4,512,3,192]{1,3,2,0:T(8,128)(2,1)} %pad_maximum_fusion.9), calls=%async_computation.3 | async-start | bytes 4718592 | tf_op jit(solution)/shard_map/while/body/eval_jaxpr/all_to_all | solution.py:213
  404.7 187.3 %copy-start.76 = (f32[768]{0:T(1024)}, f32[768]{0:T(1024)S(1)}, u32[]{:S(2)}) copy-start(f32[768]{0:T(1024)S(1)} %get-tuple-element.981) | copy-start | bytes 9220 | tf_op jit(solution)/shard_map/while
  404.7 195.1 %copy-start.35 = (f32[768]{0:T(1024)}, f32[768]{0:T(1024)S(1)}, u32[]{:S(2)}) copy-start(f32[768]{0:T(1024)S(1)} %get-tuple-element.976) | copy-start | bytes 9220 | tf_op jit(solution)/shard_map/while
  404.7 195.1 %copy-start.37 = (f32[768]{0:T(1024)}, f32[768]{0:T(1024)S(1)}, u32[]{:S(2)}) copy-start(f32[768]{0:T(1024)S(1)} %get-tuple-element.977) | copy-start | bytes 9220 | tf_op jit(solution)/shard_map/while
  416.3 41.8 %all-to-all-start = ((bf16[512,3,768]{0,1,2:T(4,128)(2,1)}), bf16[512,3,768]{0,1,2:T(4,128)(2,1)}, u32[]{:S(2)}, u32[]{:S(2)}) async-start(bf16[512,3,768]{0,1,2:T(4,128)(2,1)} %copy.76), calls=%async_computation | async-start | bytes 6291456 | tf_op jit(solution)/shard_map/while/body/eval_jaxpr/all_to_all | solution.py:165
  427.6 92.1 %copy-start.9 = (pred[512,2048]{1,0:T(8,128)(4,1)}, pred[512,2048]{1,0:T(8,128)(4,1)S(1)}, u32[]{:S(2)}) copy-start(pred[512,2048]{1,0:T(8,128)(4,1)S(1)} %get-tuple-element.842) | copy-start | bytes 3145732 | tf_op jit(solution)/shard_map/while
  427.6 111.2 %copy-start.10 = (pred[512,2048]{1,0:T(8,128)(4,1)}, pred[512,2048]{1,0:T(8,128)(4,1)S(1)}, u32[]{:S(2)}) copy-start(pred[512,2048]{1,0:T(8,128)(4,1)S(1)} %get-tuple-element.839) | copy-start | bytes 3145732 | tf_op jit(solution)/shard_map/while
  547.0 15.5 %all-to-all-start.1 = ((bf16[4,512,192]{1,2,0:T(8,128)(2,1)}), bf16[4,512,192]{1,2,0:T(8,128)(2,1)S(1)}, u32[]{:S(2)}, u32[]{:S(2)}) async-start(bf16[4,512,192]{1,2,0:T(8,128)(2,1)} %copy.79), calls=%async_computation.1 | async-start | bytes 1572864 | tf_op jit(solution)/shard_map/while/body/eval_jaxpr/all_to_all | solution.py:169
  587.6 24.3 %all-to-all-start.2 = ((bf16[512,4,192]{0,2,1:T(8,128)(2,1)}), bf16[512,4,192]{0,2,1:T(8,128)(2,1)}, u32[]{:S(2)}, u32[]{:S(2)}) async-start(bf16[512,4,192]{0,2,1:T(8,128)(2,1)} %bitcast.489), calls=%async_computation.2 | async-start | bytes 1572864 | tf_op jit(solution)/shard_map/while/body/eval_jaxpr/all_to_all | solution.py:208
  753.0 33.3 %all-to-all-start.3 = ((bf16[4,512,3,192]{1,3,2,0:T(8,128)(2,1)}), bf16[4,512,3,192]{1,3,2,0:T(8,128)(2,1)}, u32[]{:S(2)}, u32[]{:S(2)}) async-start(bf16[4,512,3,192]{1,3,2,0:T(8,128)(2,1)} %pad_maximum_fusion.9), calls=%async_computation.3 | async-start | bytes 4718592 | tf_op jit(solution)/shard_map/while/body/eval_jaxpr/all_to_all | solution.py:213
  806.5 242.4 %reduce-scatter.6.cloned.1.call-start = ((), (), s32[]{:S(2)}) async-start(), calls=%async_computation.8 | async-start | bytes 9732096 | tf_op jit(solution)/shard_map/reduce_scatter | solution.py:270
  827.2 362.9 %reduce-scatter.10.cloned.1.call-start = ((), (), s32[]{:S(2)}) async-start(), calls=%async_computation.10 | async-start | bytes 9732096 | tf_op jit(solution)/shard_map/reduce_scatter | solution.py:275
  827.9 504.0 %reduce-scatter.12.cloned.1.call-start = ((), (), s32[]{:S(2)}) async-start(), calls=%async_computation.11 | async-start | bytes 9732096 | tf_op jit(solution)/shard_map/reduce_scatter | solution.py:277
  828.0 504.0 %copy-start.1 = (bf16[3,3,768]{2,1,0:T(4,128)(2,1)S(1)}, bf16[3,3,768]{2,1,0:T(4,128)(2,1)}, u32[]{:S(2)}) copy-start(bf16[3,3,768]{2,1,0:T(4,128)(2,1)} %param.22) | copy-start | bytes 41476
  (174 other events, 1571.8 us)
Sparse Core Ops, SparseCore 0:
  806.7 100.0 reduce-scatter.7
  914.3 134.6 reduce-scatter.5
  1055.4 134.6 reduce-scatter.9
  1197.4 134.4 reduce-scatter.11
